TPU v7x, 32 devices: a whole 2x2x4 slice. The times are simulated.
32 devices in a mesh: col: 4 (over y, x), row: 8 (over z, core).
Axes of the slice: x: 2, y: 2, z: 4, core: 2. Of those that a mesh axis runs over, the one named last changes fastest.
Arguments:
- upper_blocks: float32 [4096, 512], P('row', 'col'), may hold values from -40 to 40
- lower_blocks: float32 [4096, 512], P('row', 'col'), may hold values from -40 to 40
Outputs:
- upper_rotated: float32 [4096, 512], P('row', 'col')
- lower_rotated: float32 [4096, 512], P('row', 'col')
All inputs are finite; a program needn't handle non-finite values.
Results may differ from a plain program's by a relative error of at most 0.0001.
Values sent between devices are 32-bit elements; how exact they have to be, the bound alone decides.
A program may use at most 64 MiB of HBM per device.

v0:
```python
import jax
import jax.numpy as jnp
from jax import lax
from jax.sharding import PartitionSpec as P

ROUNDS = 2


def from_behind(block, axis, distance):
    devices = range(lax.axis_size(axis))
    route = [((i - distance) % len(devices), i) for i in devices]
    return lax.ppermute(block, axis, route)


def couple(cross_gram, upper_norms, lower_norms):
    column_gap = upper_norms[..., :, None] - lower_norms[..., None, :]
    column_sum = upper_norms[..., :, None] + lower_norms[..., None, :]
    return (
        -cross_gram
        * column_gap
        / (2.0 * column_gap * column_gap + 0.5 * column_sum * column_sum + 1e-05)
    )


def rotation(coupling):
    identity = jnp.eye(coupling.shape[0], dtype=coupling.dtype)
    outer_gram = jnp.dot(coupling, coupling.T, precision=lax.Precision.HIGHEST)
    inner_gram = jnp.dot(coupling.T, coupling, precision=lax.Precision.HIGHEST)
    left_factor = jnp.linalg.cholesky(identity + outer_gram)
    right_factor = jnp.linalg.cholesky(identity + inner_gram)
    keep_upper = jax.scipy.linalg.cho_solve((left_factor, True), identity - outer_gram)
    upper_to_lower = jax.scipy.linalg.cho_solve((left_factor, True), 2.0 * coupling)
    lower_to_upper = jax.scipy.linalg.cho_solve((right_factor, True), -2.0 * coupling.T)
    keep_lower = jax.scipy.linalg.cho_solve((right_factor, True), identity - inner_gram)
    return (keep_upper, upper_to_lower, lower_to_upper, keep_lower)


def statistics(pieces):
    cross_gram = 0.0
    upper_sums = 0.0
    lower_sums = 0.0
    for entry in pieces:
        cross_gram = cross_gram + jnp.einsum(
            "rb,rd->bd", entry[0], entry[1], precision=lax.Precision.HIGHEST
        )
        upper_sums = upper_sums + jnp.sum(entry[0] * entry[0], axis=0)
        lower_sums = lower_sums + jnp.sum(entry[1] * entry[1], axis=0)
    return (cross_gram, upper_sums, lower_sums)


def rotate(first_part, second_part, from_first, from_second):
    highest = lax.Precision.HIGHEST
    return jnp.dot(first_part, from_first, precision=highest) + jnp.dot(
        second_part, from_second, precision=highest
    )


def shards(upper_blocks, lower_blocks):
    rows_dev = upper_blocks.shape[0]
    block_width = upper_blocks.shape[1]
    row_count = lax.axis_size("row")
    row_total = float(rows_dev * row_count)
    pieces = [(upper_blocks, lower_blocks)]
    for round_index in range(ROUNDS):
        cross_gram, upper_sums, lower_sums = statistics(pieces)
        shared_rows = lax.psum_scatter(cross_gram, "row", scatter_dimension=0, tiled=True)
        upper_sums, lower_sums = lax.psum((upper_sums, lower_sums), "row")
        share_rows = block_width // row_count
        first_row = lax.axis_index("row") * share_rows
        upper_share = lax.dynamic_slice_in_dim(upper_sums / row_total, first_row, share_rows)
        coupling_share = couple(shared_rows / row_total, upper_share, lower_sums / row_total)
        coupling = lax.all_gather(coupling_share, "row", axis=0, tiled=True)
        keep_upper, upper_to_lower, lower_to_upper, keep_lower = rotation(coupling)
        turned = [
            (
                rotate(entry[0], entry[1], keep_upper, lower_to_upper),
                rotate(entry[0], entry[1], upper_to_lower, keep_lower),
            )
            for entry in pieces
        ]
        if round_index + 1 < ROUNDS:
            pieces = [(from_behind(turned[0][0], "col", 1), from_behind(turned[0][1], "col", -1))]
        else:
            pieces = turned
    upper_rotated = jnp.concatenate([entry[0] for entry in pieces], axis=0)
    lower_rotated = jnp.concatenate([entry[1] for entry in pieces], axis=0)
    return (upper_rotated, lower_rotated)


def solution(mesh):
    placed = (P("row", "col"), P("row", "col"))
    return jax.shard_map(
        shards,
        mesh=mesh,
        in_specs=placed,
        out_specs=(P("row", "col"), P("row", "col")),
        check_vma=False,
    )
```

profile of v0, /device:TPU:0, one launch (start us, length us, event | category | flops | bytes accessed | tf_op | source)
XLA Modules:
  0.0 239.8 jit_solution(6282195827080017846)
XLA Ops:
  7.2 2.3 fusion.62
  9.7 0.8 copy-done
  10.5 18.1 %all-reduce.1 = (f32[128]{0:T(128)S(1)}, f32[128]{0:T(128)S(1)}) all-reduce(f32[128]{0:T(128)S(1)} %multiply_reduce_fusion.2, f32[128]{0:T(128)S(1)} %multiply_reduce_fusion.3), channel_id=1, replica_groups=mesh['col'=4,'row'=8] {'row'}, use_global_device_ids=true, to_apply=%region_4.0 | all-reduce | flops 256 | bytes 2048 | tf_op jit(solution)/shard_map/psum | solution.py:67
  28.7 15.4 %reduce-scatter.3.cloned.1.call-done = f32[16,128]{1,0:T(8,128)} async-done(((f32[128,128]{1,0:T(8,128)}), f32[16,128]{1,0:T(8,128)}) %reduce-scatter.3.cloned.1.call-update) | async-done | bytes 8208 | tf_op jit(solution)/shard_map/reduce_scatter | solution.py:66
  44.1 0.8 fusion.54
  44.9 14.0 %all_gather.6 = f32[128,128]{1,0:T(8,128)S(1)} all-gather(f32[16,128]{1,0:T(8,128)S(1)} %fusion.54), channel_id=1, replica_groups=mesh['col'=4,'row'=8] {'row'}, dimensions={0}, use_global_device_ids=true | all-gather | bytes 73728 | tf_op jit(solution)/shard_map/all_gather | solution.py:72
  59.5 11.7 %cholesky.85 = f32[128,128]{1,0:T(8,128)S(1)} custom-call(f32[128,128]{1,0:T(8,128)S(1)} %fusion.35), custom_call_target="Cholesky" | custom-call | tf_op jit(solution)/shard_map/jit(cholesky)/cholesky | solution.py:30
  71.3 0.6 compare_reduce_fusion.2
  71.9 0.7 fusion.3
  72.6 9.8 %custom-call.15 = f32[1,128,128]{1,2,0:T(8,128)S(1)} custom-call(f32[1,128,128]{2,1,0:T(8,128)S(1)} %fusion.3), custom_call_target="InvertDiagBlocksLowerTriangular" | custom-call | tf_op jit(solution)/shard_map/jit(_cho_solve)/triangular_solve | solution.py:33
  83.1 11.7 %cholesky.74 = f32[128,128]{1,0:T(8,128)S(1)} custom-call(f32[128,128]{1,0:T(8,128)S(1)} %fusion.43), custom_call_target="Cholesky" | custom-call | tf_op jit(solution)/shard_map/jit(cholesky)/cholesky | solution.py:29
  94.9 0.6 compare_reduce_fusion.3
  95.5 0.7 fusion.2
  96.2 10.0 %custom-call.14 = f32[1,128,128]{1,2,0:T(8,128)S(1)} custom-call(f32[1,128,128]{2,1,0:T(8,128)S(1)} %fusion.2), custom_call_target="InvertDiagBlocksLowerTriangular" | custom-call | tf_op jit(solution)/shard_map/jit(_cho_solve)/triangular_solve | solution.py:31
  108.0 1.5 collective-permute-start
  110.7 1.6 collective-permute-start.1
  112.3 5.8 %collective-permute-done = f32[512,128]{0,1:T(8,128)S(1)} collective-permute-done((f32[512,128]{0,1:T(8,128)S(1)}, f32[512,128]{0,1:T(8,128)S(1)}, u32[]{:S(2)}, u32[]{:S(2)}) %collective-permute-start) | collective-permute-done | bytes 262176 | tf_op jit(solution)/shard_map/ppermute | solution.py:12
  118.2 4.8 %collective-permute-done.1 = f32[512,128]{0,1:T(8,128)S(1)} collective-permute-done((f32[512,128]{0,1:T(8,128)S(1)}, f32[512,128]{0,1:T(8,128)S(1)}, u32[]{:S(2)}, u32[]{:S(2)}) %collective-permute-start.1) | collective-permute-done | bytes 262176 | tf_op jit(solution)/shard_map/ppermute | solution.py:12
  123.2 13.6 %all-reduce = (f32[128]{0:T(128)S(1)}, f32[128]{0:T(128)S(1)}) all-reduce(f32[128]{0:T(128)S(1)} %multiply_reduce_fusion, f32[128]{0:T(128)S(1)} %multiply_reduce_fusion.1), channel_id=1, replica_groups=mesh['col'=4,'row'=8] {'row'}, use_global_device_ids=true, to_apply=%region_11.14 | all-reduce | flops 256 | bytes 2048 | tf_op jit(solution)/shard_map/psum | solution.py:67
  136.8 1.0 fusion.65
  137.9 27.8 %reduce-scatter.5.cloned.1.call-done = f32[16,128]{1,0:T(8,128)} async-done(((f32[128,128]{1,0:T(8,128)}), f32[16,128]{1,0:T(8,128)}) %reduce-scatter.5.cloned.1.call-update) | async-done | bytes 8208 | tf_op jit(solution)/shard_map/reduce_scatter | solution.py:66
  165.7 0.8 fusion.57
  166.5 14.0 %all_gather.7 = f32[128,128]{1,0:T(8,128)S(1)} all-gather(f32[16,128]{1,0:T(8,128)S(1)} %fusion.57), channel_id=1, replica_groups=mesh['col'=4,'row'=8] {'row'}, dimensions={0}, use_global_device_ids=true | all-gather | bytes 73728 | tf_op jit(solution)/shard_map/all_gather | solution.py:72
  181.2 11.7 %cholesky.96 = f32[128,128]{1,0:T(8,128)S(1)} custom-call(f32[128,128]{1,0:T(8,128)S(1)} %fusion.26), custom_call_target="Cholesky" | custom-call | tf_op jit(solution)/shard_map/jit(cholesky)/cholesky | solution.py:29
  192.9 0.6 compare_reduce_fusion.1
  193.6 0.7 fusion.4
  194.2 9.8 %custom-call.18 = f32[1,128,128]{1,2,0:T(8,128)S(1)} custom-call(f32[1,128,128]{2,1,0:T(8,128)S(1)} %fusion.4), custom_call_target="InvertDiagBlocksLowerTriangular" | custom-call | tf_op jit(solution)/shard_map/jit(_cho_solve)/triangular_solve | solution.py:31
  204.8 11.7 %cholesky.107 = f32[128,128]{1,0:T(8,128)S(1)} custom-call(f32[128,128]{1,0:T(8,128)S(1)} %fusion.18), custom_call_target="Cholesky" | custom-call | tf_op jit(solution)/shard_map/jit(cholesky)/cholesky | solution.py:30
  217.1 0.7 fusion.5
  217.8 10.0 %custom-call.19 = f32[1,128,128]{1,2,0:T(8,128)S(1)} custom-call(f32[1,128,128]{2,1,0:T(8,128)S(1)} %fusion.5), custom_call_target="InvertDiagBlocksLowerTriangular" | custom-call | tf_op jit(solution)/shard_map/jit(_cho_solve)/triangular_solve | solution.py:33
  230.4 1.3 convolution_add_fusion
  231.7 1.3 convolution_add_fusion.1
  (55 shorter events, 9.8 us)
Async XLA Ops:
  7.2 2.4 %copy-start.1 = (f32[512,128]{1,0:T(8,128)S(1)}, f32[512,128]{1,0:T(8,128)}, u32[]{:S(2)}) copy-start(f32[512,128]{1,0:T(8,128)} %param.6) | copy-start | bytes 786436
  7.2 36.9 %reduce-scatter.3.cloned.1.call-start = ((), (), s32[]{:S(2)}) async-start(), calls=%async_computation.2 | async-start | bytes 73728 | tf_op jit(solution)/shard_map/reduce_scatter | solution.py:66
  9.5 0.9 copy-start
  9.5 156.2 %reduce-scatter.5.cloned.1.call-start = ((), (), s32[]{:S(2)}) async-start(), calls=%async_computation.3 | async-start | bytes 73728 | tf_op jit(solution)/shard_map/reduce_scatter | solution.py:66
  108.0 10.1 %collective-permute-start = (f32[512,128]{0,1:T(8,128)S(1)}, f32[512,128]{0,1:T(8,128)S(1)}, u32[]{:S(2)}, u32[]{:S(2)}) collective-permute-start(f32[512,128]{0,1:T(8,128)S(1)} %fusion.1), channel_id=1, source_target_pairs={{24,0},{0,8},{8,16},{16,24},{25,1},{1,9},{9,17},{17,25},{26,2},{2,... | collective-permute-start | bytes 786440 | tf_op jit(solution)/shard_map/ppermute | solution.py:12
  110.7 12.3 %collective-permute-start.1 = (f32[512,128]{0,1:T(8,128)S(1)}, f32[512,128]{0,1:T(8,128)S(1)}, u32[]{:S(2)}, u32[]{:S(2)}) collective-permute-start(f32[512,128]{0,1:T(8,128)S(1)} %fusion), channel_id=1, source_target_pairs={{8,0},{16,8},{24,16},{0,24},{9,1},{17,9},{25,17},{1,25},{10,2},{18... | collective-permute-start | bytes 786440 | tf_op jit(solution)/shard_map/ppermute | solution.py:12
Sparse Core Ops, SparseCore 0:
  10.8 33.2 reduce-scatter.2
  138.0 27.6 reduce-scatter.4
where the time goes:
time: 240 us
  other arithmetic  93.8 us (39%)
  blocking collectives  59.6 us (25%)
  waiting for transfers between devices  53.9 us (22%)
  between operations  14.4 us (6%)
  matrix products  13.8 us (6%)
  starting transfers between devices  3.11 us (1%)
    reduce_scatter x2, waiting for transfers between devices, shards(): lax.psum_scatter(cross_gram, 'row', scatter_dimension=0, tiled=True)  43.2 us
    psum x2, blocking collectives, shards(): upper_sums, lower_sums = lax.psum((upper_sums, lower_sums), 'row')  31.7 us
    all_gather x2, blocking collectives, shards(): coupling = lax.all_gather(coupling_share, 'row', axis=0, tiled=True)  28 us
    another operation x6, other arithmetic, rotation(): right_factor = jnp.linalg.cholesky(identity + inner_gram)  24.8 us
    another operation x6, other arithmetic, rotation(): left_factor = jnp.linalg.cholesky(identity + outer_gram)  24.8 us
    another operation x4, other arithmetic, rotation(): jax.scipy.linalg.cho_solve((right_factor, True), -2.0 * coupling.T)  21.1 us
    another operation x4, other arithmetic, rotation(): jax.scipy.linalg.cho_solve((left_factor, True), identity - outer_gram)  21.1 us
    ppermute x2, waiting for transfers between devices, from_behind(): return lax.ppermute(block, axis, route)  10.6 us
  transfers between devices with their start and end apart: 4, of which 4 were waited for; matrix products, arithmetic and copies ran while one was open for 1% of the time, Pallas kernels for 0%

commit v1 on v0

v1 whole, which is shorter than its diff:
```python
import functools

import jax
import jax.numpy as jnp
from jax import lax
from jax.experimental import pallas as pl
from jax.experimental.pallas import tpu as pltpu
from jax.sharding import PartitionSpec as P

ROUNDS = 2
CHUNKS = 4
MESH = pl.DeviceIdType.MESH
F32 = jnp.float32
BF16 = jnp.bfloat16
HIGHEST = lax.Precision.HIGHEST


def split(x):
    high = x.astype(BF16)
    low = (x - high.astype(F32)).astype(BF16)
    return high, low


def exact_dot(a, b, contract=(1, 0)):
    dims = (((contract[0],), (contract[1],)), ((), ()))
    return lax.dot_general(a, b, dims, precision=HIGHEST, preferred_element_type=F32)


def fast_dot(a, b):
    return jnp.dot(a, b, preferred_element_type=F32)


def gram(upper, lower):
    width = upper.shape[1]
    left = jnp.concatenate(split(upper), axis=1)
    right = jnp.concatenate(split(lower), axis=1)
    q = lax.dot_general(
        left, right, (((0,), (0,)), ((), ())), preferred_element_type=F32
    )
    return q[:width, :width] + (q[:width, width:] + q[width:, :width])


def step_count(width):
    square = (width / 4.0) ** 2
    spread = 0.5 * square / (1.0 + 0.5 * square)
    steps = 0
    while spread > 1e-3:
        spread = spread * spread / (2.0 - spread * spread)
        steps += 1
    return steps


def rotation(p):
    width = p.shape[0]
    rows = lax.broadcasted_iota(jnp.int32, (width, width), 0)
    lanes = lax.broadcasted_iota(jnp.int32, (width, width), 1)
    eye = (rows == lanes).astype(F32)
    s = exact_dot(p, p, (1, 1))
    total = jnp.sum(jnp.sum(p * p, axis=0, keepdims=True), axis=1, keepdims=True)
    total = jnp.broadcast_to(total, (1, width))
    scale = 1.0 / (1.0 + 0.5 * total)
    spread = 0.5 * total * scale
    e = spread * eye - scale * s
    x = None
    steps = step_count(width)
    for step in range(steps):
        square = spread * spread
        gain = 2.0 / (2.0 - square)
        spread = 0.5 * square * gain
        if step == 0:
            x = (gain * scale) * (eye + e)
            squared = exact_dot(e, e)
        elif step < steps - 1:
            y = exact_dot(jnp.concatenate([x, e], axis=0), e)
            x = gain * (x + y[:width])
            squared = y[width:]
        else:
            x = gain * (x + exact_dot(x, e))
        if step < steps - 1:
            e = gain * squared - spread * eye
    e = (eye - x) - exact_dot(s, x)
    x = x + exact_dot(x, e)
    ap = exact_dot(x, p)
    cross = 2.0 * ap
    keep_upper = 2.0 * x - eye
    keep_lower = eye - exact_dot(p, cross, (0, 0))
    top = jnp.concatenate([keep_upper, cross], axis=1)
    bottom = jnp.concatenate([-cross.T, keep_lower], axis=1)
    return jnp.concatenate([top, bottom], axis=0)


def turn(upper, lower, parts):
    high, low = split(jnp.concatenate([upper, lower], axis=1))
    w_high, w_low = parts
    return fast_dot(high, w_high) + (fast_dot(low, w_high) + fast_dot(high, w_low))


def kernel(
    n_row, n_col, upper_ref, lower_ref, out_upper, out_lower,
    swapped, work, gram_out, gram_in, line_out, line_in, pair,
    swap_send, swap_recv, gram_send, gram_recv, line_send, line_recv,
    pair_send, pair_recv, shift_send, shift_recv,
):
    depth, width = upper_ref.shape
    half = width // 2
    chunk = depth // CHUNKS
    n_line = n_row // 2
    row_total = float(depth * n_row)
    row, col = lax.axis_index("row"), lax.axis_index("col")
    core = lax.rem(row, 2)
    chip_row = row - core
    partner = chip_row + 1 - core
    odd = lax.rem(col, 2)
    beside = col + 1 - 2 * odd
    ahead = lax.rem(col + 2, n_col)
    behind = lax.rem(col + n_col - 2, n_col)
    shift_to = ahead + odd * (behind - ahead)

    def line_row(k):
        return lax.rem(row + 2 * k, n_row)

    barrier = pltpu.get_barrier_semaphore()
    greeted = [(chip_row, beside), (chip_row + 1, beside), (partner, col)]
    greeted += [(line_row(k), col) for k in range(1, n_line)]
    greeted += [(row, ahead)] + ([] if n_col == 4 else [(row, behind)])
    for r, c in greeted:
        pl.semaphore_signal(barrier, inc=1, device_id={"row": r, "col": c}, device_id_type=MESH)

    def remote(src, dst, send, recv, r, c):
        return pltpu.make_async_remote_copy(
            src_ref=src, dst_ref=dst, send_sem=send, recv_sem=recv,
            device_id={"row": r, "col": c}, device_id_type=MESH,
        )

    def put_statistics(index, g, upper_sums, lower_sums):
        which = lax.broadcasted_iota(jnp.int32, (8, width), 0)
        norms = jnp.where(which == 0, upper_sums, jnp.where(which == 1, lower_sums, 0.0))
        for k in range(2):
            gram_out[index, k, :half, :] = g[k * half : (k + 1) * half]
            gram_out[index, k, half:, :] = norms

    def reduce_line(index, own):
        line_out[index] = own
        copies = []
        for k in range(1, n_line):
            copies.append(
                remote(
                    line_out.at[index], line_in.at[index, k - 1],
                    line_send.at[index, k - 1], line_recv.at[index, k - 1], line_row(k), col,
                )
            )
            copies[-1].start()
        total = own
        for k in range(1, n_line):
            copies[k - 1].wait_recv()
            total = total + line_in[index, k - 1]
        return total, copies

    def coupling(index, total):
        total = total / row_total
        a_row, b = total[half : half + 1], total[half + 1 : half + 2]
        i = lax.broadcasted_iota(jnp.int32, (half, width), 0) + core * half
        j = lax.broadcasted_iota(jnp.int32, (half, width), 1)
        a = jnp.sum(jnp.where(i == j, a_row, 0.0), axis=1, keepdims=True)
        gap, both = a - b, a + b
        share = -total[:half] * gap / (2.0 * gap * gap + 0.5 * both * both + 1e-05)
        pair[index, core] = share
        copy = remote(
            pair.at[index, core], pair.at[index, core],
            pair_send.at[index], pair_recv.at[index], partner, col,
        )
        copy.start()
        copy.wait_recv()
        return pair[index].reshape(width, width), copy

    pending = []

    upper, lower = upper_ref[...], lower_ref[...]
    put_statistics(
        0, gram(upper, lower),
        jnp.sum(upper * upper, axis=0, keepdims=True), jnp.sum(lower * lower, axis=0, keepdims=True),
    )
    pl.semaphore_wait(barrier, len(greeted))

    copies = []
    for k in range(2):
        copies.append(
            remote(
                gram_out.at[0, k], gram_in.at[core], gram_send.at[k], gram_recv.at[core],
                chip_row + k, beside,
            )
        )
        copies[-1].start()
    pending += copies
    swaps = []
    for i in range(CHUNKS):
        rows = pl.ds(i * chunk, chunk)
        for which, ref in enumerate((upper_ref, lower_ref)):
            swaps.append(
                remote(
                    ref.at[rows], swapped.at[which, rows],
                    swap_send.at[which, i], swap_recv.at[which, i], row, beside,
                )
            )
            swaps[-1].start()
    pending += swaps
    for k in range(2):
        pltpu.make_async_remote_copy(
            src_ref=gram_out.at[0, k], dst_ref=gram_in.at[k], send_sem=gram_send.at[k],
            recv_sem=gram_recv.at[k], device_id={"row": row, "col": beside}, device_id_type=MESH,
        ).wait_recv()
    total, copies = reduce_line(0, gram_in[0] + gram_in[1])
    pending += copies
    p, copy = coupling(0, total)
    pending.append(copy)
    parts = split(rotation(p))

    shifts = []
    for i in range(CHUNKS):
        rows = pl.ds(i * chunk, chunk)
        swaps[2 * i].wait_recv()
        swaps[2 * i + 1].wait_recv()
        y = turn(swapped[0, rows, :], swapped[1, rows, :], parts)
        work[0, rows, :] = y[:, :width]
        work[1, rows, :] = y[:, width:]
        shifts.append(
            remote(
                work.at[odd, rows], work.at[2, rows], shift_send.at[i], shift_recv.at[i],
                row, shift_to,
            )
        )
        shifts[-1].start()
    pending += shifts

    upper_slot, lower_slot = 2 - 2 * odd, 1 + odd
    g, upper_sums, lower_sums = 0.0, 0.0, 0.0
    for i in range(CHUNKS):
        rows = pl.ds(i * chunk, chunk)
        shifts[i].wait_recv()
        upper, lower = work[upper_slot, rows, :], work[lower_slot, rows, :]
        g = g + gram(upper, lower)
        upper_sums = upper_sums + jnp.sum(upper * upper, axis=0, keepdims=True)
        lower_sums = lower_sums + jnp.sum(lower * lower, axis=0, keepdims=True)
    put_statistics(1, g, upper_sums, lower_sums)
    copy = remote(
        gram_out.at[1, 1 - core], gram_in.at[2], gram_send.at[2], gram_recv.at[2], partner, col
    )
    copy.start()
    pending.append(copy)
    copy.wait_recv()
    total, copies = reduce_line(1, gram_out[1, core] + gram_in[2])
    pending += copies
    p, copy = coupling(1, total)
    pending.append(copy)
    parts = split(rotation(p))
    for i in range(CHUNKS):
        rows = pl.ds(i * chunk, chunk)
        y = turn(work[upper_slot, rows, :], work[lower_slot, rows, :], parts)
        out_upper[rows, :] = y[:, :width]
        out_lower[rows, :] = y[:, width:]
    for copy in pending:
        copy.wait_send()


def shards(n_row, n_col, upper_blocks, lower_blocks):
    depth, width = upper_blocks.shape
    half = width // 2
    n_line = n_row // 2
    out = jax.ShapeDtypeStruct((depth, width), F32)
    dma = pltpu.SemaphoreType.DMA
    return pl.pallas_call(
        functools.partial(kernel, n_row, n_col),
        out_shape=(out, out),
        in_specs=[pl.BlockSpec(memory_space=pltpu.VMEM)] * 2,
        out_specs=(pl.BlockSpec(memory_space=pltpu.VMEM),) * 2,
        scratch_shapes=[
            pltpu.VMEM((2, depth, width), F32),
            pltpu.VMEM((3, depth, width), F32),
            pltpu.VMEM((ROUNDS, 2, half + 8, width), F32),
            pltpu.VMEM((3, half + 8, width), F32),
            pltpu.VMEM((ROUNDS, half + 8, width), F32),
            pltpu.VMEM((ROUNDS, n_line - 1, half + 8, width), F32),
            pltpu.VMEM((ROUNDS, 2, half, width), F32),
            dma((2, CHUNKS)),
            dma((2, CHUNKS)),
            dma((3,)),
            dma((3,)),
            dma((ROUNDS, n_line - 1)),
            dma((ROUNDS, n_line - 1)),
            dma((ROUNDS,)),
            dma((ROUNDS,)),
            dma((CHUNKS,)),
            dma((CHUNKS,)),
        ],
        compiler_params=pltpu.CompilerParams(collective_id=0, has_side_effects=True),
    )(upper_blocks, lower_blocks)


def solution(mesh):
    placed = (P("row", "col"), P("row", "col"))
    return jax.shard_map(
        functools.partial(shards, mesh.shape["row"], mesh.shape["col"]),
        mesh=mesh,
        in_specs=placed,
        out_specs=(P("row", "col"), P("row", "col")),
        check_vma=False,
    )
```

time: 240 us -> 42.5 us (0.18)
  other arithmetic: 93.8 us -> 0 us
  blocking collectives: 59.6 us -> 0 us
  waiting for transfers between devices: 53.9 us -> 0 us
  Pallas kernels: 0 us -> 39.2 us
  matrix products: 13.8 us -> 0 us
  between operations: 14.4 us -> 0.65 us
  starting transfers between devices: 3.11 us -> 0 us
    another operation x20 -> x0, other arithmetic: 91.7 us -> none  [the longest x6 24.8 us: rotation(): right_factor = jnp.linalg.cholesky(identity + inner_gram)]
    reduce_scatter x2 -> x0, waiting for transfers between devices: 43.2 us -> none  [shards(): lax.psum_scatter(cross_gram, 'row', scatter_dimension=0, tiled=True)]
    pallas_call x0 -> x1, Pallas kernels: none -> 39.2 us  [shards(): pl.pallas_call(functools.partial(kernel, n_row, n_col), out_shape=(out, o...]
    psum x2 -> x0, blocking collectives: 31.7 us -> none  [shards(): upper_sums, lower_sums = lax.psum((upper_sums, lower_sums), 'row')]
    all_gather x2 -> x0, blocking collectives: 28 us -> none  [shards(): coupling = lax.all_gather(coupling_share, 'row', axis=0, tiled=True)]
    ppermute x2 -> x0, waiting for transfers between devices: 10.6 us -> none  [from_behind(): return lax.ppermute(block, axis, route)]
    dot_general x14 -> x0, matrix products: 9.86 us -> none  [the longest x4 3.43 us: rotate(): jnp.dot(first_part, from_first, precision=highest)]
    another operation x16 -> x0, matrix products: 3.9 us -> none  [the longest x4 0.98 us: rotation(): jax.scipy.linalg.cho_solve((left_factor, True), 2.0 * coupling)]
  transfers between devices with their start and end apart: 4 -> 0, of which waited for: 4 -> 0; matrix products, arithmetic and copies ran while one was open for 1% -> 0% of each run, Pallas kernels for 0% -> 0%
where the time goes in v1:
time: 42.5 us; the launch traced here: 42.3 us
  Pallas kernels  39.2 us (92%)
  local copies, waits for them, and re-layouts  2.42 us (6%)
  between operations  0.65 us (2%)
    pallas_call x1, Pallas kernels, shards(): pl.pallas_call(functools.partial(kernel, n_row, n_col), out_shape=(out, o...  39.2 us
    unnamed x4, local copies, waits for them, and re-layouts  2.42 us

profile of v1, /device:TPU:0, one launch (start us, length us, event | category | flops | bytes accessed | tf_op | source)
XLA Modules:
  0.0 42.3 jit_solution(10523221584501880538)
XLA Ops:
  0.6 39.2 %shard_map.41 = (f32[512,128]{1,0:T(8,128)}, f32[512,128]{1,0:T(8,128)}) custom-call(f32[512,128]{1,0:T(8,128)} %upper_ref.1, f32[512,128]{1,0:T(8,128)} %lower_ref.1), custom_call_target="tpu_custom_call" | custom-call | tf_op jit(solution)/shard_map/pallas_call | solution.py:271
  39.8 0.0 copy-start
  39.8 1.7 %copy.6 = f32[512,128]{1,0:T(8,128)} copy(f32[512,128]{1,0:T(8,128)} %get-tuple-element.4) | data formatting | bytes 524288
  41.6 0.0 copy-done
  41.6 0.7 %copy.7 = f32[512,128]{1,0:T(8,128)} copy(f32[512,128]{1,0:T(8,128)S(1)} %copy-done) | data formatting | bytes 524288
Async XLA Ops:
  39.8 1.7 %copy-start = (f32[512,128]{1,0:T(8,128)S(1)}, f32[512,128]{1,0:T(8,128)}, u32[]{:S(2)}) copy-start(f32[512,128]{1,0:T(8,128)} %get-tuple-element.5) | copy-start | bytes 786436

commit v2 on v1

--- a/solution.py
+++ b/solution.py
@@ -12,7 +12,6 @@
 MESH = pl.DeviceIdType.MESH
 F32 = jnp.float32
 BF16 = jnp.bfloat16
-HIGHEST = lax.Precision.HIGHEST
 
 
 def split(x):
@@ -21,13 +20,25 @@
     return high, low
 
 
-def exact_dot(a, b, contract=(1, 0)):
-    dims = (((contract[0],), (contract[1],)), ((), ()))
-    return lax.dot_general(a, b, dims, precision=HIGHEST, preferred_element_type=F32)
+def split_three(x):
+    high = x.astype(BF16)
+    rest = x - high.astype(F32)
+    middle = rest.astype(BF16)
+    return high, middle, (rest - middle.astype(F32)).astype(BF16)
 
 
 def fast_dot(a, b):
     return jnp.dot(a, b, preferred_element_type=F32)
+
+
+def exact_dot(a, b):
+    width = b.shape[1]
+    (a0, a1, a2), (b0, b1, b2) = split_three(a), split_three(b)
+    upper = jnp.concatenate([b0, b1], axis=1)
+    lower = jnp.concatenate([b1, b0], axis=1)
+    large = fast_dot(jnp.concatenate([a0, a1], axis=1), jnp.concatenate([upper, lower], axis=0))
+    small = fast_dot(jnp.concatenate([a0, a2], axis=1), jnp.concatenate([b2, b0], axis=0))
+    return large[:, :width] + (large[:, width:] + small)
 
 
 def gram(upper, lower):
@@ -55,7 +66,7 @@
     rows = lax.broadcasted_iota(jnp.int32, (width, width), 0)
     lanes = lax.broadcasted_iota(jnp.int32, (width, width), 1)
     eye = (rows == lanes).astype(F32)
-    s = exact_dot(p, p, (1, 1))
+    s = exact_dot(p, p.T)
     total = jnp.sum(jnp.sum(p * p, axis=0, keepdims=True), axis=1, keepdims=True)
     total = jnp.broadcast_to(total, (1, width))
     scale = 1.0 / (1.0 + 0.5 * total)
@@ -83,7 +94,7 @@
     ap = exact_dot(x, p)
     cross = 2.0 * ap
     keep_upper = 2.0 * x - eye
-    keep_lower = eye - exact_dot(p, cross, (0, 0))
+    keep_lower = eye - exact_dot(p.T, cross)
     top = jnp.concatenate([keep_upper, cross], axis=1)
     bottom = jnp.concatenate([-cross.T, keep_lower], axis=1)
     return jnp.concatenate([top, bottom], axis=0)
@@ -96,12 +107,13 @@
 
 
 def kernel(
-    n_row, n_col, upper_ref, lower_ref, out_upper, out_lower,
-    swapped, work, gram_out, gram_in, line_out, line_in, pair,
+    n_row, n_col, upper_hbm, lower_hbm, work, out_p,
+    loaded, swapped, gram_out, gram_in, line_out, line_in, pair,
     swap_send, swap_recv, gram_send, gram_recv, line_send, line_recv,
-    pair_send, pair_recv, shift_send, shift_recv,
+    pair_send, pair_recv, shift_send, shift_recv, load_sem,
 ):
-    depth, width = upper_ref.shape
+    depth, width = upper_hbm.shape
+    upper_ref, lower_ref = loaded.at[0], loaded.at[1]
     half = width // 2
     chunk = depth // CHUNKS
     n_line = n_row // 2
@@ -119,6 +131,12 @@
     def line_row(k):
         return lax.rem(row + 2 * k, n_row)
 
+    loads = []
+    for i in range(CHUNKS):
+        rows = pl.ds(i * chunk, chunk)
+        for which, ref in enumerate((upper_hbm, lower_hbm)):
+            loads.append(pltpu.make_async_copy(ref.at[rows], loaded.at[which, rows], load_sem.at[which, i]))
+            loads[-1].start()
     barrier = pltpu.get_barrier_semaphore()
     greeted = [(chip_row, beside), (chip_row + 1, beside), (partner, col)]
     greeted += [(line_row(k), col) for k in range(1, n_line)]
@@ -175,11 +193,21 @@
 
     pending = []
 
-    upper, lower = upper_ref[...], lower_ref[...]
-    put_statistics(
-        0, gram(upper, lower),
-        jnp.sum(upper * upper, axis=0, keepdims=True), jnp.sum(lower * lower, axis=0, keepdims=True),
-    )
+    def statistics(index, fetch):
+        g, upper_sums, lower_sums = 0.0, 0.0, 0.0
+        for i in range(CHUNKS):
+            upper, lower = fetch(i, pl.ds(i * chunk, chunk))
+            g = g + gram(upper, lower)
+            upper_sums = upper_sums + jnp.sum(upper * upper, axis=0, keepdims=True)
+            lower_sums = lower_sums + jnp.sum(lower * lower, axis=0, keepdims=True)
+        put_statistics(index, g, upper_sums, lower_sums)
+
+    def fetch_loaded(i, rows):
+        loads[2 * i].wait()
+        loads[2 * i + 1].wait()
+        return loaded[0, rows, :], loaded[1, rows, :]
+
+    statistics(0, fetch_loaded)
     pl.semaphore_wait(barrier, len(greeted))
 
     copies = []
@@ -233,15 +261,12 @@
     pending += shifts
 
     upper_slot, lower_slot = 2 - 2 * odd, 1 + odd
-    g, upper_sums, lower_sums = 0.0, 0.0, 0.0
-    for i in range(CHUNKS):
-        rows = pl.ds(i * chunk, chunk)
+
+    def fetch_shifted(i, rows):
         shifts[i].wait_recv()
-        upper, lower = work[upper_slot, rows, :], work[lower_slot, rows, :]
-        g = g + gram(upper, lower)
-        upper_sums = upper_sums + jnp.sum(upper * upper, axis=0, keepdims=True)
-        lower_sums = lower_sums + jnp.sum(lower * lower, axis=0, keepdims=True)
-    put_statistics(1, g, upper_sums, lower_sums)
+        return work[upper_slot, rows, :], work[lower_slot, rows, :]
+
+    statistics(1, fetch_shifted)
     copy = remote(
         gram_out.at[1, 1 - core], gram_in.at[2], gram_send.at[2], gram_recv.at[2], partner, col
     )
@@ -252,14 +277,27 @@
     pending += copies
     p, copy = coupling(1, total)
     pending.append(copy)
-    parts = split(rotation(p))
+    out_p[...] = p
+    for copy in pending:
+        copy.wait_send()
+
+
+def finish(work, p_ref, out_upper, out_lower, stage, sems):
+    depth, width = out_upper.shape
+    chunk = depth // CHUNKS
+    odd = lax.rem(lax.axis_index("col"), 2)
+    upper_slot, lower_slot = 2 - 2 * odd, 1 + odd
+    parts = split(rotation(p_ref[...]))
+    copies = []
     for i in range(CHUNKS):
         rows = pl.ds(i * chunk, chunk)
         y = turn(work[upper_slot, rows, :], work[lower_slot, rows, :], parts)
-        out_upper[rows, :] = y[:, :width]
-        out_lower[rows, :] = y[:, width:]
-    for copy in pending:
-        copy.wait_send()
+        for which, out in enumerate((out_upper, out_lower)):
+            stage[which, rows, :] = y[:, which * width : (which + 1) * width]
+            copies.append(pltpu.make_async_copy(stage.at[which, rows], out.at[rows], sems.at[which, i]))
+            copies[-1].start()
+    for copy in copies:
+        copy.wait()
 
 
 def shards(n_row, n_col, upper_blocks, lower_blocks):
@@ -268,14 +306,14 @@
     n_line = n_row // 2
     out = jax.ShapeDtypeStruct((depth, width), F32)
     dma = pltpu.SemaphoreType.DMA
-    return pl.pallas_call(
+    work, p = pl.pallas_call(
         functools.partial(kernel, n_row, n_col),
-        out_shape=(out, out),
-        in_specs=[pl.BlockSpec(memory_space=pltpu.VMEM)] * 2,
+        out_shape=(pltpu.VMEM((3, depth, width), F32), pltpu.VMEM((width, width), F32)),
+        in_specs=[pl.BlockSpec(memory_space=pl.ANY)] * 2,
         out_specs=(pl.BlockSpec(memory_space=pltpu.VMEM),) * 2,
         scratch_shapes=[
             pltpu.VMEM((2, depth, width), F32),
-            pltpu.VMEM((3, depth, width), F32),
+            pltpu.VMEM((2, depth, width), F32),
             pltpu.VMEM((ROUNDS, 2, half + 8, width), F32),
             pltpu.VMEM((3, half + 8, width), F32),
             pltpu.VMEM((ROUNDS, half + 8, width), F32),
@@ -291,9 +329,17 @@
             dma((ROUNDS,)),
             dma((CHUNKS,)),
             dma((CHUNKS,)),
+            dma((2, CHUNKS)),
         ],
         compiler_params=pltpu.CompilerParams(collective_id=0, has_side_effects=True),
     )(upper_blocks, lower_blocks)
+    return pl.pallas_call(
+        finish,
+        out_shape=(out, out),
+        in_specs=[pl.BlockSpec(memory_space=pltpu.VMEM)] * 2,
+        out_specs=(pl.BlockSpec(memory_space=pl.ANY),) * 2,
+        scratch_shapes=[pltpu.VMEM((2, depth, width), F32), dma((2, CHUNKS))],
+    )(*(pltpu.with_memory_space_constraint(x, pltpu.VMEM) for x in (work, p)))
 
 
 def solution(mesh):

time: 42.5 us -> 37.6 us (0.88)
  Pallas kernels: 39.2 us -> 36.7 us
  local copies, waits for them, and re-layouts: 2.42 us -> 0 us
    pallas_call x1 -> x2, Pallas kernels: 39.2 us -> 36.7 us  [the longest x1 33.3 us: shards(): pl.pallas_call(functools.partial(kernel, n_row, n_col), out_shape=(pltpu....]
    unnamed x4 -> x0, local copies, waits for them, and re-layouts: 2.42 us -> none
where the time goes in v2:
time: 37.6 us; the launch traced here: 37.4 us
  Pallas kernels  36.7 us (98%)
  between operations  0.64 us (2%)
    pallas_call x1, Pallas kernels, shards(): pl.pallas_call(functools.partial(kernel, n_row, n_col), out_shape=(pltpu....  33.3 us
    pallas_call x1, Pallas kernels, shards(): pl.pallas_call(finish, out_shape=(out, out), in_specs=[pl.BlockSpec(memor...  3.49 us

profile of v2, /device:TPU:0, one launch (start us, length us, event | category | flops | bytes accessed | tf_op | source)
XLA Modules:
  0.0 37.4 jit_solution(5212499355159537256)
XLA Ops:
  0.6 33.3 %shard_map.41 = (f32[3,512,128]{2,1,0:T(8,128)S(1)}, f32[128,128]{1,0:T(8,128)S(1)}) custom-call(f32[512,128]{1,0:T(8,128)} %upper_hbm.1, f32[512,128]{1,0:T(8,128)} %lower_hbm.1), custom_call_target="tpu_custom_call" | custom-call | tf_op jit(solution)/shard_map/pallas_call | solution.py:309
  33.9 3.5 %shard_map.42 = (f32[512,128]{1,0:T(8,128)}, f32[512,128]{1,0:T(8,128)}) custom-call(f32[3,512,128]{2,1,0:T(8,128)S(1)} %get-tuple-element.4.work, f32[128,128]{1,0:T(8,128)S(1)} %get-tuple-element.5.p_ref), custom_call_target="tpu_custom_call" | custom-call | tf_op jit(solution)/shard_map/pallas_call | solution.py:336

commit v3 on v2

--- a/solution.py
+++ b/solution.py
@@ -8,7 +8,10 @@
 from jax.sharding import PartitionSpec as P
 
 ROUNDS = 2
-CHUNKS = 4
+LOADS = 2
+SWAPS = 2
+SHIFTS = 4
+STORES = 4
 MESH = pl.DeviceIdType.MESH
 F32 = jnp.float32
 BF16 = jnp.bfloat16
@@ -82,9 +85,8 @@
             x = (gain * scale) * (eye + e)
             squared = exact_dot(e, e)
         elif step < steps - 1:
-            y = exact_dot(jnp.concatenate([x, e], axis=0), e)
-            x = gain * (x + y[:width])
-            squared = y[width:]
+            squared = exact_dot(e, e)
+            x = gain * (x + exact_dot(x, e))
         else:
             x = gain * (x + exact_dot(x, e))
         if step < steps - 1:
@@ -115,7 +117,6 @@
     depth, width = upper_hbm.shape
     upper_ref, lower_ref = loaded.at[0], loaded.at[1]
     half = width // 2
-    chunk = depth // CHUNKS
     n_line = n_row // 2
     row_total = float(depth * n_row)
     row, col = lax.axis_index("row"), lax.axis_index("col")
@@ -131,9 +132,12 @@
     def line_row(k):
         return lax.rem(row + 2 * k, n_row)
 
+    def piece(i, count):
+        return pl.ds(i * (depth // count), depth // count)
+
     loads = []
-    for i in range(CHUNKS):
-        rows = pl.ds(i * chunk, chunk)
+    for i in range(LOADS):
+        rows = piece(i, LOADS)
         for which, ref in enumerate((upper_hbm, lower_hbm)):
             loads.append(pltpu.make_async_copy(ref.at[rows], loaded.at[which, rows], load_sem.at[which, i]))
             loads[-1].start()
@@ -193,10 +197,10 @@
 
     pending = []
 
-    def statistics(index, fetch):
+    def statistics(index, count, fetch):
         g, upper_sums, lower_sums = 0.0, 0.0, 0.0
-        for i in range(CHUNKS):
-            upper, lower = fetch(i, pl.ds(i * chunk, chunk))
+        for i in range(count):
+            upper, lower = fetch(i, piece(i, count))
             g = g + gram(upper, lower)
             upper_sums = upper_sums + jnp.sum(upper * upper, axis=0, keepdims=True)
             lower_sums = lower_sums + jnp.sum(lower * lower, axis=0, keepdims=True)
@@ -207,7 +211,7 @@
         loads[2 * i + 1].wait()
         return loaded[0, rows, :], loaded[1, rows, :]
 
-    statistics(0, fetch_loaded)
+    statistics(0, LOADS, fetch_loaded)
     pl.semaphore_wait(barrier, len(greeted))
 
     copies = []
@@ -221,8 +225,8 @@
         copies[-1].start()
     pending += copies
     swaps = []
-    for i in range(CHUNKS):
-        rows = pl.ds(i * chunk, chunk)
+    for i in range(SWAPS):
+        rows = piece(i, SWAPS)
         for which, ref in enumerate((upper_ref, lower_ref)):
             swaps.append(
                 remote(
@@ -244,10 +248,11 @@
     parts = split(rotation(p))
 
     shifts = []
-    for i in range(CHUNKS):
-        rows = pl.ds(i * chunk, chunk)
-        swaps[2 * i].wait_recv()
-        swaps[2 * i + 1].wait_recv()
+    for i in range(SHIFTS):
+        rows = piece(i, SHIFTS)
+        if i % (SHIFTS // SWAPS) == 0:
+            swaps[2 * (i * SWAPS // SHIFTS)].wait_recv()
+            swaps[2 * (i * SWAPS // SHIFTS) + 1].wait_recv()
         y = turn(swapped[0, rows, :], swapped[1, rows, :], parts)
         work[0, rows, :] = y[:, :width]
         work[1, rows, :] = y[:, width:]
@@ -266,7 +271,7 @@
         shifts[i].wait_recv()
         return work[upper_slot, rows, :], work[lower_slot, rows, :]
 
-    statistics(1, fetch_shifted)
+    statistics(1, SHIFTS, fetch_shifted)
     copy = remote(
         gram_out.at[1, 1 - core], gram_in.at[2], gram_send.at[2], gram_recv.at[2], partner, col
     )
@@ -284,12 +289,12 @@
 
 def finish(work, p_ref, out_upper, out_lower, stage, sems):
     depth, width = out_upper.shape
-    chunk = depth // CHUNKS
+    chunk = depth // STORES
     odd = lax.rem(lax.axis_index("col"), 2)
     upper_slot, lower_slot = 2 - 2 * odd, 1 + odd
     parts = split(rotation(p_ref[...]))
     copies = []
-    for i in range(CHUNKS):
+    for i in range(STORES):
         rows = pl.ds(i * chunk, chunk)
         y = turn(work[upper_slot, rows, :], work[lower_slot, rows, :], parts)
         for which, out in enumerate((out_upper, out_lower)):
@@ -319,17 +324,17 @@
             pltpu.VMEM((ROUNDS, half + 8, width), F32),
             pltpu.VMEM((ROUNDS, n_line - 1, half + 8, width), F32),
             pltpu.VMEM((ROUNDS, 2, half, width), F32),
-            dma((2, CHUNKS)),
-            dma((2, CHUNKS)),
+            dma((2, SWAPS)),
+            dma((2, SWAPS)),
             dma((3,)),
             dma((3,)),
             dma((ROUNDS, n_line - 1)),
             dma((ROUNDS, n_line - 1)),
             dma((ROUNDS,)),
             dma((ROUNDS,)),
-            dma((CHUNKS,)),
-            dma((CHUNKS,)),
-            dma((2, CHUNKS)),
+            dma((SHIFTS,)),
+            dma((SHIFTS,)),
+            dma((2, LOADS)),
         ],
         compiler_params=pltpu.CompilerParams(collective_id=0, has_side_effects=True),
     )(upper_blocks, lower_blocks)
@@ -338,7 +343,7 @@
         out_shape=(out, out),
         in_specs=[pl.BlockSpec(memory_space=pltpu.VMEM)] * 2,
         out_specs=(pl.BlockSpec(memory_space=pl.ANY),) * 2,
-        scratch_shapes=[pltpu.VMEM((2, depth, width), F32), dma((2, CHUNKS))],
+        scratch_shapes=[pltpu.VMEM((2, depth, width), F32), dma((2, STORES))],
     )(*(pltpu.with_memory_space_constraint(x, pltpu.VMEM) for x in (work, p)))
 
 

time: 37.6 us -> 37 us (0.984)
  Pallas kernels: 36.7 us -> 36.3 us
where the time goes in v3:
time: 37 us; the launch traced here: 36.9 us
  Pallas kernels  36.3 us (98%)
  between operations  0.64 us (2%)
    pallas_call x1, Pallas kernels, shards(): pl.pallas_call(functools.partial(kernel, n_row, n_col), out_shape=(pltpu....  32.9 us
    pallas_call x1, Pallas kernels, shards(): pl.pallas_call(finish, out_shape=(out, out), in_specs=[pl.BlockSpec(memor...  3.35 us

profile of v3, /device:TPU:0, one launch (start us, length us, event | category | flops | bytes accessed | tf_op | source)
XLA Modules:
  0.0 36.9 jit_solution(5002164208186937373)
XLA Ops:
  0.6 32.9 %shard_map.41 = (f32[3,512,128]{2,1,0:T(8,128)S(1)}, f32[128,128]{1,0:T(8,128)S(1)}) custom-call(f32[512,128]{1,0:T(8,128)} %upper_hbm.1, f32[512,128]{1,0:T(8,128)} %lower_hbm.1), custom_call_target="tpu_custom_call" | custom-call | tf_op jit(solution)/shard_map/pallas_call | solution.py:314
  33.5 3.3 %shard_map.42 = (f32[512,128]{1,0:T(8,128)}, f32[512,128]{1,0:T(8,128)}) custom-call(f32[3,512,128]{2,1,0:T(8,128)S(1)} %get-tuple-element.4.work, f32[128,128]{1,0:T(8,128)S(1)} %get-tuple-element.5.p_ref), custom_call_target="tpu_custom_call" | custom-call | tf_op jit(solution)/shard_map/pallas_call | solution.py:341

commit v4 on v3

--- a/solution.py
+++ b/solution.py
@@ -179,21 +179,20 @@
         return total, copies
 
     def coupling(index, total):
-        total = total / row_total
-        a_row, b = total[half : half + 1], total[half + 1 : half + 2]
-        i = lax.broadcasted_iota(jnp.int32, (half, width), 0) + core * half
-        j = lax.broadcasted_iota(jnp.int32, (half, width), 1)
-        a = jnp.sum(jnp.where(i == j, a_row, 0.0), axis=1, keepdims=True)
-        gap, both = a - b, a + b
-        share = -total[:half] * gap / (2.0 * gap * gap + 0.5 * both * both + 1e-05)
-        pair[index, core] = share
+        pair[index, core] = total[:half]
         copy = remote(
             pair.at[index, core], pair.at[index, core],
             pair_send.at[index], pair_recv.at[index], partner, col,
         )
         copy.start()
+        norms = total[half:] / row_total
+        a_row, b = norms[:1], norms[1:2]
+        a = jnp.broadcast_to(a_row, (width, width)).T
+        gap, both = a - b, a + b
+        factor = -gap / (2.0 * gap * gap + 0.5 * both * both + 1e-05)
         copy.wait_recv()
-        return pair[index].reshape(width, width), copy
+        cross_gram = pair[index].reshape(width, width) / row_total
+        return cross_gram * factor, copy
 
     pending = []
 

time: 37 us -> 36.9 us (level)
  no operation moved by 1% of the time
where the time goes in v4:
time: 36.9 us; the launch traced here: 36.7 us
  Pallas kernels  36.1 us (98%)
  between operations  0.64 us (2%)
    pallas_call x1, Pallas kernels, shards(): pl.pallas_call(functools.partial(kernel, n_row, n_col), out_shape=(pltpu....  32.7 us
    pallas_call x1, Pallas kernels, shards(): pl.pallas_call(finish, out_shape=(out, out), in_specs=[pl.BlockSpec(memor...  3.35 us

profile of v4, /device:TPU:0, one launch (start us, length us, event | category | flops | bytes accessed | tf_op | source)
XLA Modules:
  0.0 36.7 jit_solution(8773783502434847293)
XLA Ops:
  0.6 32.7 %shard_map.41 = (f32[3,512,128]{2,1,0:T(8,128)S(1)}, f32[128,128]{1,0:T(8,128)S(1)}) custom-call(f32[512,128]{1,0:T(8,128)} %upper_hbm.1, f32[512,128]{1,0:T(8,128)} %lower_hbm.1), custom_call_target="tpu_custom_call" | custom-call | tf_op jit(solution)/shard_map/pallas_call | solution.py:313
  33.4 3.4 %shard_map.42 = (f32[512,128]{1,0:T(8,128)}, f32[512,128]{1,0:T(8,128)}) custom-call(f32[3,512,128]{2,1,0:T(8,128)S(1)} %get-tuple-element.4.work, f32[128,128]{1,0:T(8,128)S(1)} %get-tuple-element.5.p_ref), custom_call_target="tpu_custom_call" | custom-call | tf_op jit(solution)/shard_map/pallas_call | solution.py:340
